TPU v7x, 256 devices: a whole 4x4x8 slice. The times are simulated.
256 devices in a mesh: dp: 4 (over y), mp: 64 (over x, z, core).
Axes of the slice: x: 4, y: 4, z: 8, core: 2. Of those that a mesh axis runs over, the one named last changes fastest.
Arguments:
- inputs: bfloat16 [8, 256, 6144], P('dp', None, 'mp'), may hold values from -6 to 6
- cotangent: bfloat16 [8, 256, 6144], P('dp', None, 'mp'), may hold values from -6 to 6
- w_up: bfloat16 [6144, 24576], P('dp', 'mp'), may hold values from -0.078125 to 0.078125
- w_down: bfloat16 [24576, 6144], P('mp', 'dp'), may hold values from -0.0390625 to 0.0390625
- thresholds: float32 [2], replicated, may hold values from 23592.96 to 58982.4
Outputs:
- grad_up: float32 [6144, 24576], P('dp', 'mp')
- grad_down: float32 [24576, 6144], P('mp', 'dp')
- norms: float32 [8, 2], P('dp')
All inputs are finite; a program needn't handle non-finite values.
Results may differ from a plain program's by a relative error of at most 0.0085.
Values may be sent and summed in bfloat16 or wider, within the bound.
A program may use at most 128 MiB of HBM per device.

v0:
```python
import jax
import jax.numpy as jnp
from jax import lax
from jax.sharding import PartitionSpec as P

inv_root_two = 0.7071067811865476
inv_root_two_pi = 0.3989422804014327


def sent_to_all(shard, axis):
    copies = jnp.broadcast_to(shard, (lax.axis_size(axis), *shard.shape))
    return lax.all_to_all(copies, axis, split_axis=0, concat_axis=0, tiled=True)


def taken_together(shard, axis):
    return sent_to_all(shard, axis).sum(axis=0)


def packed_total(arrays, axis):
    line, at, outs = (jnp.concatenate([a.reshape(-1) for a in arrays]), 0, [])
    running = taken_together(line, axis)
    for a in arrays:
        outs.append(running[at : at + a.size].reshape(a.shape))
        at += a.size
    return tuple(outs)


def split_up(shard, dim, count):
    shape = shard.shape
    pieces = shard.reshape(*shape[:dim], count, shape[dim] // count, *shape[dim + 1 :])
    return jnp.moveaxis(pieces, dim, 0)


def sum_at_owner(shard, axis, dim):
    pieces = split_up(shard, dim, lax.axis_size(axis))
    arrived = lax.all_to_all(pieces, axis, split_axis=0, concat_axis=0, tiled=True)
    return arrived.astype(jnp.float32).sum(axis=0)


def normal_cdf(value):
    return 0.5 * (1.0 + lax.erf(value * inv_root_two))


def gram_of(array, images, patches):
    cube = array.reshape(images, patches, -1)
    return jnp.einsum("btd,bsd->bts", cube, cube, preferred_element_type=jnp.float32)


def on_device(inputs, cotangent, w_up, w_down, thresholds):
    images, patches, local_feats = inputs.shape
    count_rows = images * patches
    x_whole = lax.all_gather(inputs, "mp", axis=2, tiled=True).reshape(count_rows, -1)
    hidden_local = w_up.shape[1]
    columns = x_whole
    pre = jnp.dot(
        columns, lax.all_gather(w_up, "dp", axis=0, tiled=True), preferred_element_type=jnp.float32
    )
    act = (pre * normal_cdf(pre)).astype(jnp.bfloat16)
    dy_whole = lax.all_gather(cotangent, "mp", axis=2, tiled=True).reshape(count_rows, -1)
    columns = dy_whole
    dact = lax.dot_general(
        columns,
        lax.all_gather(w_down, "dp", axis=1, tiled=True),
        (((1,), (1,)), ((), ())),
        preferred_element_type=jnp.float32,
    )
    slope = normal_cdf(pre) + pre * jnp.exp(-0.5 * pre * pre) * inv_root_two_pi
    dpre = (dact * slope).astype(jnp.bfloat16)
    gram_dpre = gram_of(dpre, images, patches)
    gram_act = gram_of(act, images, patches)
    part_up = jnp.sum(gram_of(x_whole, images, patches) * gram_dpre, axis=(1, 2))
    part_down = jnp.sum(gram_act * gram_of(dy_whole, images, patches), axis=(1, 2))
    sq_up, sq_down = packed_total((part_up, part_down), "mp")
    norms = jnp.stack([jnp.sqrt(sq_up), jnp.sqrt(sq_down)], axis=1)
    factor = jnp.minimum(1.0, thresholds[None, :] / (norms + 1e-06))
    dpre_clip = (
        (
            factor[:, 0][:, None, None]
            * dpre.reshape(images, patches, hidden_local).astype(jnp.float32)
        )
        .astype(jnp.bfloat16)
        .reshape(count_rows, hidden_local)
    )
    cot_clip = (
        (factor[:, 1][:, None, None] * dy_whole.reshape(images, patches, -1).astype(jnp.float32))
        .astype(jnp.bfloat16)
        .reshape(count_rows, -1)
    )
    columns = x_whole
    grad_up = lax.psum_scatter(
        lax.dot_general(
            columns, dpre_clip, (((0,), (0,)), ((), ())), preferred_element_type=jnp.float32
        ).astype(jnp.bfloat16),
        "dp",
        scatter_dimension=0,
        tiled=True,
    ).astype(jnp.float32)
    down_full = lax.dot_general(
        act, cot_clip, (((0,), (0,)), ((), ())), preferred_element_type=jnp.float32
    )
    grad_down = sum_at_owner(down_full.astype(jnp.bfloat16), "dp", 1)
    return (grad_up, grad_down, norms)


def solution(mesh):
    in_specs = (P("dp", None, "mp"), P("dp", None, "mp"), P("dp", "mp"), P("mp", "dp"), P())
    out_specs = (P("dp", "mp"), P("mp", "dp"), P("dp", None))
    return jax.shard_map(
        on_device, mesh=mesh, in_specs=in_specs, out_specs=out_specs, check_vma=False
    )
```

profile of v0, /device:TPU:1, one launch (start us, length us, event | category | flops | bytes accessed | tf_op | source)
XLA Modules:
  0.0 445.1 jit_solution(11769768210793305239)
XLA Ops:
  7.2 0.0 all-gather.5.cloned.1.call-start
  7.2 0.7 all-gather.5.cloned.1.call-update
  7.9 0.0 all-gather.7.cloned.1.call-start
  7.9 0.7 all-gather.7.cloned.1.call-update
  8.6 0.0 all-gather.11.cloned.1.call-start
  8.7 0.7 all-gather.11.cloned.1.call-update
  9.4 0.0 all-gather.9.cloned.1.call-start
  9.4 0.5 all-gather.9.cloned.1.call-update
  10.0 85.6 %all-gather.5.cloned.1.call-done = bf16[2,256,6144]{1,2,0:T(8,128)(2,1)} async-done(((bf16[2,256,96]{1,2,0:T(8,128)(2,1)}), bf16[2,256,6144]{1,2,0:T(8,128)(2,1)}) %all-gather.5.cloned.1.call-update) | async-done | bytes 6291472 | tf_op jit(solution)/shard_map/all_gather | solution.py:52
  95.5 8.7 %copy.32 = bf16[2,256,6144]{2,1,0:T(8,128)(2,1)} copy(bf16[2,256,6144]{1,2,0:T(8,128)(2,1)} %all-gather.5.cloned.1.call-done) | data formatting | bytes 12582912 | tf_op jit(solution)/shard_map/all_gather | solution.py:52
  104.2 71.4 %all-gather.7.cloned.1.call-done = bf16[2,256,6144]{1,2,0:T(8,128)(2,1)} async-done(((bf16[2,256,96]{1,2,0:T(8,128)(2,1)}), bf16[2,256,6144]{1,2,0:T(8,128)(2,1)}) %all-gather.7.cloned.1.call-update) | async-done | bytes 6291472 | tf_op jit(solution)/shard_map/all_gather | solution.py:59
  175.6 8.7 %copy.31 = bf16[2,256,6144]{2,1,0:T(8,128)(2,1)} copy(bf16[2,256,6144]{1,2,0:T(8,128)(2,1)} %all-gather.7.cloned.1.call-done) | data formatting | bytes 12582912 | tf_op jit(solution)/shard_map/all_gather | solution.py:59
  184.3 44.5 %all-gather.11.cloned.1.call-done = bf16[6144,384]{1,0:T(8,128)(2,1)} async-done(((bf16[1536,384]{1,0:T(8,128)(2,1)}), bf16[6144,384]{1,0:T(8,128)(2,1)}) %all-gather.11.cloned.1.call-update) | async-done | bytes 4718608 | tf_op jit(solution)/shard_map/all_gather | solution.py:56
  228.8 7.0 %multiply_convert_fusion.2 = (bf16[512,384]{1,0:T(8,128)(2,1)S(1)}, f32[512,384]{1,0:T(8,128)S(1)}) fusion(bf16[512,6144]{1,0:T(8,128)(2,1)} %bitcast.47, bf16[6144,384]{1,0:T(8,128)(2,1)} %all-gather.11.cloned.1.call-done), kind=kOutput, calls=%fused_computation.18 | convolution fusion | flops 2416902144 | bytes 12189696 | tf_op jit(solution)/shard_map/dot_general | solution.py:55
  235.7 50.3 %all-gather.9.cloned.1.call-done = bf16[384,6144]{1,0:T(8,128)(2,1)} async-done(((bf16[384,1536]{1,0:T(8,128)(2,1)}), bf16[384,6144]{1,0:T(8,128)(2,1)}) %all-gather.9.cloned.1.call-update) | async-done | bytes 4718608 | tf_op jit(solution)/shard_map/all_gather | solution.py:63
  286.0 7.7 %fusion.1 = bf16[512,384]{1,0:T(8,128)(2,1)S(1)} fusion(bf16[512,6144]{1,0:T(8,128)(2,1)} %bitcast.46, bf16[384,6144]{1,0:T(8,128)(2,1)} %all-gather.9.cloned.1.call-done, f32[512,384]{1,0:T(8,128)S(1)} %get-tuple-element.25), kind=kOutput, calls=%fused_computation.7 | convolution fusion | flops 2417885184 | bytes 12189696 | tf_op jit(solution)/shard_map/dot_general | solution.py:61
  293.7 0.3 fusion.9
  294.0 0.0 slice-start
  294.0 0.3 fusion.10
  294.4 0.0 slice-start.1
  294.4 7.4 %fusion.2 = f32[2]{0:T(128)S(1)} fusion(f32[2,256,256]{2,1,0:T(8,128)S(1)} %fusion.9, bf16[2,256,6144]{1,2,0:T(8,128)(2,1)} %all-gather.5.cloned.1.call-done), kind=kOutput, calls=%fused_computation.11 | convolution fusion | flops 1610874880 | bytes 6815752 | tf_op jit(solution)/shard_map/btd,bsd->bts/dot_general | solution.py:46
  301.8 0.0 slice-done
  301.8 0.0 slice-done.1
  301.8 0.0 copy-start
  301.8 2.7 fusion.3
  304.5 0.1 pad_maximum_fusion.1
  304.6 0.6 broadcast_in_dim.4
  305.2 10.8 %all-to-all-start = ((f32[64,1,4]{2,1,0:T(1,128)}), f32[64,1,4]{2,1,0:T(1,128)S(1)}, u32[]{:S(2)}, u32[]{:S(2)}) async-start(f32[64,1,4]{2,1,0:T(1,128)} %broadcast_in_dim.4), calls=%async_computation | async-start | bytes 65536 | tf_op jit(solution)/shard_map/all_to_all | solution.py:12
  316.1 0.2 reduce-scatter.2.cloned.1.call-start
  316.3 0.2 copy.34
  316.5 8.8 %all-to-all-done = f32[64,1,4]{2,1,0:T(1,128)S(1)} async-done(((f32[64,1,4]{2,1,0:T(1,128)}), f32[64,1,4]{2,1,0:T(1,128)S(1)}, u32[]{:S(2)}, u32[]{:S(2)}) %all-to-all-start) | async-done | bytes 1056 | tf_op jit(solution)/shard_map/all_to_all | solution.py:12
  325.3 0.1 reduce_sum.38
  325.4 0.1 sqrt_bitcast_fusion.1
  325.5 0.0 copy-done
  325.5 0.1 pad_maximum_fusion
  325.5 8.6 %fusion = bf16[6144,384]{0,1:T(8,128)(2,1)} fusion(bf16[2,256,6144]{1,2,0:T(8,128)(2,1)} %all-gather.5.cloned.1.call-done, bf16[2,256,384]{1,2,0:T(8,128)(2,1)S(1)} %copy.34, f32[2]{0:T(128)S(1)} %get-tuple-element.21), kind=kOutput, calls=%fused_computation.4 | convolution fusion | flops 2418868224 | bytes 11403272 | tf_op jit(solution)/shard_map/dot_general | solution.py:91
  334.2 0.0 reduce-scatter.2.cloned.1.call-update
  334.2 7.5 %multiply_convert_fusion = bf16[2,256,6144]{1,2,0:T(8,128)(2,1)} fusion(bf16[2,256,6144]{1,2,0:T(8,128)(2,1)} %all-gather.7.cloned.1.call-done, f32[2]{0:T(128)S(1)} %get-tuple-element.20), kind=kLoop, calls=%fused_computation | loop fusion | flops 9437184 | bytes 12582920 | tf_op jit(solution)/shard_map/convert_element_type | solution.py:86
  341.7 8.7 %copy.35 = bf16[2,256,6144]{2,1,0:T(8,128)(2,1)} copy(bf16[2,256,6144]{1,2,0:T(8,128)(2,1)} %multiply_convert_fusion) | data formatting | bytes 12582912 | tf_op jit(solution)/shard_map/convert_element_type | solution.py:86
  350.4 5.4 %convolution_convert_fusion = bf16[384,6144]{1,0:T(8,128)(2,1)S(1)} fusion(bf16[512,384]{1,0:T(8,128)(2,1)S(1)} %get-tuple-element.24, bf16[512,6144]{1,0:T(8,128)(2,1)} %bitcast.43), kind=kOutput, calls=%fused_computation.3 | convolution fusion | flops 2418278400 | bytes 11403264 | tf_op jit(solution)/shard_map/dot_general | solution.py:98
  355.8 2.6 copy.44
  358.4 4.9 %all-to-all-start.1 = ((bf16[4,384,1536]{2,1,0:T(8,128)(2,1)}), bf16[4,384,1536]{2,1,0:T(8,128)(2,1)}, u32[]{:S(2)}, u32[]{:S(2)}) async-start(bf16[4,384,1536]{2,1,0:T(8,128)(2,1)} %bitcast.44), calls=%async_computation.2 | async-start | bytes 9437184 | tf_op jit(solution)/shard_map/all_to_all | solution.py:36
  363.3 0.6 copy.38
  364.0 67.2 %all-to-all-done.1 = bf16[4,384,1536]{2,1,0:T(8,128)(2,1)} async-done(((bf16[4,384,1536]{2,1,0:T(8,128)(2,1)}), bf16[4,384,1536]{2,1,0:T(8,128)(2,1)}, u32[]{:S(2)}, u32[]{:S(2)}) %all-to-all-start.1) | async-done | bytes 4718624 | tf_op jit(solution)/shard_map/all_to_all | solution.py:36
  431.2 4.7 %convert_reduce_fusion = f32[384,1536]{1,0:T(8,128)} fusion(bf16[4,384,1536]{2,1,0:T(8,128)(2,1)} %all-to-all-done.1), kind=kLoop, calls=%fused_computation.2 | loop fusion | flops 4128768 | bytes 7077888 | tf_op jit(solution)/shard_map/reduce_sum | solution.py:37
  435.9 0.0 reduce-scatter.2.cloned.1.call-done
  435.9 2.7 copy.37
  (2 shorter events, 0.0 us)
Async XLA Ops:
  7.2 88.4 %all-gather.5.cloned.1.call-start = ((), (), s32[]{:S(2)}) async-start(), calls=%async_computation.3 | async-start | bytes 6389760 | tf_op jit(solution)/shard_map/all_gather | solution.py:52
  7.9 167.7 %all-gather.7.cloned.1.call-start = ((), (), s32[]{:S(2)}) async-start(), calls=%async_computation.4 | async-start | bytes 6389760 | tf_op jit(solution)/shard_map/all_gather | solution.py:59
  8.6 220.1 %all-gather.11.cloned.1.call-start = ((), (), s32[]{:S(2)}) async-start(), calls=%async_computation.6 | async-start | bytes 5898240 | tf_op jit(solution)/shard_map/all_gather | solution.py:56
  9.4 276.6 %all-gather.9.cloned.1.call-start = ((), (), s32[]{:S(2)}) async-start(), calls=%async_computation.5 | async-start | bytes 5898240 | tf_op jit(solution)/shard_map/all_gather | solution.py:63
  294.0 7.8 %slice-start = ((s8[6291456]{0:T(1024)(128)(4,1)}), s8[4194304]{0:T(1024)(128)(4,1)S(1)}, s32[]{:S(2)}) async-start(s8[6291456]{0:T(1024)(128)(4,1)} %bitcast.41), calls=%async_computation.8 | async-start | bytes 8388608
  294.4 7.4 %slice-start.1 = ((s8[6291456]{0:T(1024)(128)(4,1)}), s8[2097152]{0:T(1024)(128)(4,1)S(1)}, s32[]{:S(2)}) async-start(s8[6291456]{0:T(1024)(128)(4,1)} %bitcast.41), calls=%async_computation.9 | async-start | bytes 4194304
  301.8 23.7 %copy-start = (f32[2]{0:T(128)S(1)}, f32[2]{0:T(128)}, u32[]{:S(2)}) copy-start(f32[2]{0:T(128)} %param.9) | copy-start | bytes 28
  305.2 20.1 %all-to-all-start = ((f32[64,1,4]{2,1,0:T(1,128)}), f32[64,1,4]{2,1,0:T(1,128)S(1)}, u32[]{:S(2)}, u32[]{:S(2)}) async-start(f32[64,1,4]{2,1,0:T(1,128)} %broadcast_in_dim.4), calls=%async_computation | async-start | bytes 65536 | tf_op jit(solution)/shard_map/all_to_all | solution.py:12
  316.1 119.8 %reduce-scatter.2.cloned.1.call-start = ((), (), s32[]{:S(2)}) async-start(), calls=%async_computation.7 | async-start | bytes 5898240 | tf_op jit(solution)/shard_map/reduce_scatter | solution.py:90
  358.4 72.8 %all-to-all-start.1 = ((bf16[4,384,1536]{2,1,0:T(8,128)(2,1)}), bf16[4,384,1536]{2,1,0:T(8,128)(2,1)}, u32[]{:S(2)}, u32[]{:S(2)}) async-start(bf16[4,384,1536]{2,1,0:T(8,128)(2,1)} %bitcast.44), calls=%async_computation.2 | async-start | bytes 9437184 | tf_op jit(solution)/shard_map/all_to_all | solution.py:36
Sparse Core Ops, SparseCore 0:
  10.8 84.6 all-gather.4
  98.3 77.2 all-gather.6
  177.4 51.2 all-gather.10
  230.4 55.5 all-gather.8
  334.3 59.8 reduce-scatter.1
where the time goes:
time: 446 us; the launch traced here: 445 us
  waiting for transfers between devices  330 us (74%)
  matrix products  39.5 us (9%)
  local copies, waits for them, and re-layouts  32.9 us (7%)
  starting transfers between devices  16.1 us (4%)
  between operations  13.9 us (3%)
  other arithmetic  12.4 us (3%)
    all_gather x1, waiting for transfers between devices, on_device(): lax.all_gather(inputs, 'mp', axis=2, tiled=True).reshape(count_rows, -1)  85.6 us
    all_gather x1, waiting for transfers between devices, on_device(): lax.all_gather(cotangent, 'mp', axis=2, tiled=True).reshape(count_rows, -1)  71.4 us
    all_to_all x1, waiting for transfers between devices, sum_at_owner(): lax.all_to_all(pieces, axis, split_axis=0, concat_axis=0, tiled=True)  67.2 us
    all_gather x1, waiting for transfers between devices, on_device(): lax.all_gather(w_down, 'dp', axis=1, tiled=True)  50.3 us
    all_gather x1, waiting for transfers between devices, on_device(): lax.all_gather(w_up, 'dp', axis=0, tiled=True)  44.5 us
    all_to_all x1, starting transfers between devices, sent_to_all(): return lax.all_to_all(copies, axis, split_axis=0, concat_axis=0, tiled=True)  10.8 us
    dot_general x4, matrix products, gram_of(): jnp.einsum('btd,bsd->bts', cube, cube, preferred_element_type=jnp.float32)  10.8 us
  transfers between devices with their start and end apart: 7, of which 6 were waited for; matrix products, arithmetic and copies ran while one was open for 12% of the time, Pallas kernels for 0%

commit v1 on v0

--- a/solution.py
+++ b/solution.py
@@ -5,6 +5,11 @@
 
 inv_root_two = 0.7071067811865476
 inv_root_two_pi = 0.3989422804014327
+
+
+def gather_from_all(shard, axis, dim):
+    copies = jnp.concatenate([shard] * lax.axis_size(axis), axis=dim)
+    return lax.all_to_all(copies, axis, dim, dim, tiled=True)
 
 
 def sent_to_all(shard, axis):
@@ -49,7 +54,7 @@
 def on_device(inputs, cotangent, w_up, w_down, thresholds):
     images, patches, local_feats = inputs.shape
     count_rows = images * patches
-    x_whole = lax.all_gather(inputs, "mp", axis=2, tiled=True).reshape(count_rows, -1)
+    x_whole = gather_from_all(inputs, "mp", 2).reshape(count_rows, -1)
     hidden_local = w_up.shape[1]
     columns = x_whole
     pre = jnp.dot(

time: 446 us -> 419 us (0.939)
  waiting for transfers between devices: 330 us -> 209 us
  local copies, waits for them, and re-layouts: 32.9 us -> 103 us
  blocking collectives: 0 us -> 14.9 us
    all_to_all x1, waiting for transfers between devices: 8.83 us -> 139 us  [gather_from_all(): return lax.all_to_all(copies, axis, dim, dim, tiled=True)]
    all_gather x1 -> x0, waiting for transfers between devices: 85.6 us -> none  [on_device(): lax.all_gather(inputs, 'mp', axis=2, tiled=True).reshape(count_rows, -1)]
    unnamed x8 -> x75, local copies, waits for them, and re-layouts: 3.37 us -> 82.3 us
    all_gather x1, waiting for transfers between devices: 71.4 us -> 0.01 us  [on_device(): lax.all_gather(cotangent, 'mp', axis=2, tiled=True).reshape(count_rows, -1)]
    all_gather x1, waiting for transfers between devices: 50.3 us -> 0.01 us  [on_device(): lax.all_gather(w_down, 'dp', axis=1, tiled=True)]
    all_gather x1, waiting for transfers between devices: 44.5 us -> 0.01 us  [on_device(): lax.all_gather(w_up, 'dp', axis=0, tiled=True)]
    all_to_all x0 -> x1, blocking collectives: none -> 14.9 us  [sent_to_all(): return lax.all_to_all(copies, axis, split_axis=0, concat_axis=0, tiled=True)]
    all_gather x1 -> x0, local copies, waits for them, and re-layouts: 8.67 us -> none  [on_device(): lax.all_gather(inputs, 'mp', axis=2, tiled=True).reshape(count_rows, -1)]
  transfers between devices with their start and end apart: 7 -> 6, of which waited for: 6 -> 2; matrix products, arithmetic and copies ran while one was open for 12% -> 33% of each run, Pallas kernels for 0% -> 0%
where the time goes in v1:
time: 419 us; the launch traced here: 417 us
  waiting for transfers between devices  209 us (50%)
  local copies, waits for them, and re-layouts  103 us (25%)
  matrix products  42 us (10%)
  starting transfers between devices  18.5 us (4%)
  other arithmetic  15.3 us (4%)
  blocking collectives  14.9 us (4%)
  between operations  13.9 us (3%)
    all_to_all x1, waiting for transfers between devices, gather_from_all(): return lax.all_to_all(copies, axis, dim, dim, tiled=True)  139 us
    unnamed x75, local copies, waits for them, and re-layouts  82.3 us
    all_to_all x1, waiting for transfers between devices, sum_at_owner(): lax.all_to_all(pieces, axis, split_axis=0, concat_axis=0, tiled=True)  68.1 us
    all_to_all x1, blocking collectives, sent_to_all(): return lax.all_to_all(copies, axis, split_axis=0, concat_axis=0, tiled=True)  14.9 us
    all_to_all x1, starting transfers between devices, gather_from_all(): return lax.all_to_all(copies, axis, dim, dim, tiled=True)  13.1 us
    dot_general x4, matrix products, gram_of(): jnp.einsum('btd,bsd->bts', cube, cube, preferred_element_type=jnp.float32)  11.6 us
    all_gather x1, local copies, waits for them, and re-layouts, on_device(): lax.all_gather(cotangent, 'mp', axis=2, tiled=True).reshape(count_rows, -1)  8.74 us
    convert_element_type x1, local copies, waits for them, and re-layouts, on_device(): cot_clip = (factor[:, 1][:, None, None] * dy_whole.reshape(images, patche...  8.72 us
  transfers between devices with their start and end apart: 6, of which 2 were waited for; matrix products, arithmetic and copies ran while one was open for 33% of the time, Pallas kernels for 0%

profile of v1, /device:TPU:1, one launch (start us, length us, event | category | flops | bytes accessed | tf_op | source)
XLA Modules:
  0.0 417.0 jit_solution(13515267550333373807)
XLA Ops:
  7.9 1.6 constant_dynamic-update-slice_fusion.63
  9.6 1.6 constant_dynamic-update-slice_fusion.62
  11.2 1.6 constant_dynamic-update-slice_fusion.61
  12.8 1.6 constant_dynamic-update-slice_fusion.60
  14.5 1.6 constant_dynamic-update-slice_fusion.59
  16.1 1.6 constant_dynamic-update-slice_fusion.58
  17.7 1.6 constant_dynamic-update-slice_fusion.57
  19.4 1.6 constant_dynamic-update-slice_fusion.56
  21.0 1.6 constant_dynamic-update-slice_fusion.55
  22.6 1.6 constant_dynamic-update-slice_fusion.54
  24.3 1.6 constant_dynamic-update-slice_fusion.53
  25.9 1.6 constant_dynamic-update-slice_fusion.52
  27.5 1.6 constant_dynamic-update-slice_fusion.51
  29.2 1.6 constant_dynamic-update-slice_fusion.50
  30.8 1.6 constant_dynamic-update-slice_fusion.49
  32.4 1.6 constant_dynamic-update-slice_fusion.48
  34.1 1.6 constant_dynamic-update-slice_fusion.47
  35.7 1.6 constant_dynamic-update-slice_fusion.46
  37.3 1.6 constant_dynamic-update-slice_fusion.45
  40.6 1.6 constant_dynamic-update-slice_fusion.43
  42.2 1.6 constant_dynamic-update-slice_fusion.42
  43.9 1.6 constant_dynamic-update-slice_fusion.41
  45.5 1.6 constant_dynamic-update-slice_fusion.40
  47.1 1.6 constant_dynamic-update-slice_fusion.39
  48.8 1.6 constant_dynamic-update-slice_fusion.38
  50.4 1.6 constant_dynamic-update-slice_fusion.37
  52.0 1.6 constant_dynamic-update-slice_fusion.36
  53.7 1.6 constant_dynamic-update-slice_fusion.35
  55.3 1.6 constant_dynamic-update-slice_fusion.34
  58.6 1.6 constant_dynamic-update-slice_fusion.32
  83.9 13.1 %all-to-all-start = ((bf16[2,256,6144]{1,0,2:T(2,128)(2,1)}), bf16[2,256,6144]{1,0,2:T(2,128)(2,1)}, u32[]{:S(2)}, u32[]{:S(2)}) async-start(bf16[2,256,6144]{1,0,2:T(2,128)(2,1)} %constant_dynamic-update-slice_fusion), calls=%async_computation | async-start | bytes 12582912 | tf_op jit(solution)/shard_map/all_to_all | solution.py:12
  98.8 139.1 %all-to-all-done = bf16[2,256,6144]{1,0,2:T(2,128)(2,1)} async-done(((bf16[2,256,6144]{1,0,2:T(2,128)(2,1)}), bf16[2,256,6144]{1,0,2:T(2,128)(2,1)}, u32[]{:S(2)}, u32[]{:S(2)}) %all-to-all-start) | async-done | bytes 6291488 | tf_op jit(solution)/shard_map/all_to_all | solution.py:12
  237.9 6.4 %copy.360 = bf16[768,8,2,256]{3,1,2,0:T(8,128)(2,1)} copy(bf16[768,8,2,256]{3,2,1,0:T(2,128)(2,1)} %bitcast.13) | data formatting | bytes 12582912
  244.3 8.7 %copy.350 = bf16[2,256,6144]{2,1,0:T(8,128)(2,1)} copy(bf16[2,256,6144]{1,2,0:T(8,128)(2,1)} %all-gather.4.cloned.1.call-done) | data formatting | bytes 12582912 | tf_op jit(solution)/shard_map/all_gather | solution.py:64
  253.1 8.5 %multiply_convert_fusion.2 = (bf16[512,384]{1,0:T(8,128)(2,1)S(1)}, f32[512,384]{1,0:T(8,128)}) fusion(bf16[512,6144]{0,1:T(8,128)(2,1)} %bitcast.39, bf16[6144,384]{1,0:T(8,128)(2,1)} %all-gather.8.cloned.1.call-done), kind=kOutput, calls=%fused_computation.20 | convolution fusion | flops 2416902144 | bytes 12189696 | tf_op jit(solution)/shard_map/dot_general | solution.py:60
  261.9 8.3 %fusion = f32[2,256,256]{2,1,0:T(8,128)} fusion(bf16[2,256,6144]{1,0,2:T(2,128)(2,1)} %all-to-all-done), kind=kOutput, calls=%fused_computation.4 | convolution fusion | flops 1610612736 | bytes 6815744 | tf_op jit(solution)/shard_map/btd,bsd->bts/dot_general | solution.py:51
  270.1 8.0 %fusion.3 = bf16[512,384]{1,0:T(8,128)(2,1)S(1)} fusion(bf16[512,6144]{1,0:T(8,128)(2,1)} %bitcast.43, bf16[384,6144]{1,0:T(8,128)(2,1)} %all-gather.6.cloned.1.call-done, f32[512,384]{1,0:T(8,128)} %get-tuple-element.25), kind=kOutput, calls=%fused_computation.9 | convolution fusion | flops 2417885184 | bytes 12189696 | tf_op jit(solution)/shard_map/dot_general | solution.py:66
  278.6 2.6 fusion.5
  281.3 14.9 %all_to_all.16 = f32[64,1,4]{2,1,0:T(1,128)S(1)} all-to-all(f32[64,1,4]{2,1,0:T(1,128)S(1)} %broadcast_in_dim.4), channel_id=1, replica_groups=mesh['dp'=4,'mp'=64] {'mp'}, dimensions={0} | all-to-all | bytes 2048 | tf_op jit(solution)/shard_map/all_to_all | solution.py:17
  296.5 8.4 %bitcast_convert_fusion = bf16[6144,384]{1,0:T(8,128)(2,1)} fusion(bf16[2,256,6144]{1,0,2:T(2,128)(2,1)} %all-to-all-done, bf16[2,256,384]{2,1,0:T(8,128)(2,1)S(1)} %bitcast.46, f32[2]{0:T(128)S(1)} %get-tuple-element.21), kind=kOutput, calls=%fused_computation.1 | convolution fusion | flops 2418868224 | bytes 11403272 | tf_op jit(solution)/shard_map/dot_general | solution.py:96
  304.9 7.6 %multiply_convert_fusion = bf16[2,256,6144]{1,2,0:T(8,128)(2,1)} fusion(bf16[2,256,6144]{1,2,0:T(8,128)(2,1)} %all-gather.4.cloned.1.call-done, f32[2]{0:T(128)S(1)} %get-tuple-element.20), kind=kLoop, calls=%fused_computation | loop fusion | flops 9437184 | bytes 12582920 | tf_op jit(solution)/shard_map/convert_element_type | solution.py:91
  312.5 8.7 %copy.353 = bf16[2,256,6144]{2,1,0:T(8,128)(2,1)} copy(bf16[2,256,6144]{1,2,0:T(8,128)(2,1)} %multiply_convert_fusion) | data formatting | bytes 12582912 | tf_op jit(solution)/shard_map/convert_element_type | solution.py:91
  321.2 5.5 %convolution_convert_fusion = bf16[384,6144]{1,0:T(8,128)(2,1)S(1)} fusion(bf16[512,384]{1,0:T(8,128)(2,1)S(1)} %get-tuple-element.24, bf16[512,6144]{1,0:T(8,128)(2,1)} %bitcast.40), kind=kOutput, calls=%fused_computation.3 | convolution fusion | flops 2418278400 | bytes 11403264 | tf_op jit(solution)/shard_map/dot_general | solution.py:103
  326.7 2.5 copy.430
  329.3 5.0 %all-to-all-start.2 = ((bf16[4,384,1536]{2,1,0:T(8,128)(2,1)}), bf16[4,384,1536]{2,1,0:T(8,128)(2,1)}, u32[]{:S(2)}, u32[]{:S(2)}) async-start(bf16[4,384,1536]{2,1,0:T(8,128)(2,1)} %bitcast.41), calls=%async_computation.3 | async-start | bytes 9437184 | tf_op jit(solution)/shard_map/all_to_all | solution.py:41
  334.9 68.1 %all-to-all-done.2 = bf16[4,384,1536]{2,1,0:T(8,128)(2,1)} async-done(((bf16[4,384,1536]{2,1,0:T(8,128)(2,1)}), bf16[4,384,1536]{2,1,0:T(8,128)(2,1)}, u32[]{:S(2)}, u32[]{:S(2)}) %all-to-all-start.2) | async-done | bytes 4718624 | tf_op jit(solution)/shard_map/all_to_all | solution.py:41
  403.0 4.7 %convert_reduce_fusion = f32[384,1536]{1,0:T(8,128)} fusion(bf16[4,384,1536]{2,1,0:T(8,128)(2,1)} %all-to-all-done.2), kind=kLoop, calls=%fused_computation.2 | loop fusion | flops 4128768 | bytes 7077888 | tf_op jit(solution)/shard_map/reduce_sum | solution.py:42
  407.7 2.8 convert_element_type.35
  (66 shorter events, 31.1 us)
Async XLA Ops:
  7.2 53.1 %copy-start = (bf16[2,256,96]{1,2,0:T(8,128)(2,1)S(1)}, bf16[2,256,96]{1,2,0:T(8,128)(2,1)}, u32[]{:S(2)}) copy-start(bf16[2,256,96]{1,2,0:T(8,128)(2,1)} %param.5) | copy-start | bytes 294916
  7.2 237.1 %all-gather.4.cloned.1.call-start = ((), (), s32[]{:S(2)}) async-start(), calls=%async_computation.4 | async-start | bytes 6389760 | tf_op jit(solution)/shard_map/all_gather | solution.py:64
  83.9 154.0 %all-to-all-start = ((bf16[2,256,6144]{1,0,2:T(2,128)(2,1)}), bf16[2,256,6144]{1,0,2:T(2,128)(2,1)}, u32[]{:S(2)}, u32[]{:S(2)}) async-start(bf16[2,256,6144]{1,0,2:T(2,128)(2,1)} %constant_dynamic-update-slice_fusion), calls=%async_computation | async-start | bytes 12582912 | tf_op jit(solution)/shard_map/all_to_all | solution.py:12
  97.1 156.0 %all-gather.8.cloned.1.call-start = ((), (), s32[]{:S(2)}) async-start(), calls=%async_computation.6 | async-start | bytes 5898240 | tf_op jit(solution)/shard_map/all_gather | solution.py:61
  97.8 172.3 %all-gather.6.cloned.1.call-start = ((), (), s32[]{:S(2)}) async-start(), calls=%async_computation.5 | async-start | bytes 5898240 | tf_op jit(solution)/shard_map/all_gather | solution.py:68
  98.5 309.1 %reduce-scatter.2.cloned.1.call-start = ((), (), s32[]{:S(2)}) async-start(), calls=%async_computation.7 | async-start | bytes 5898240 | tf_op jit(solution)/shard_map/reduce_scatter | solution.py:95
  261.9 16.7 %slice-start = ((s8[6291456]{0:T(1024)(128)(4,1)}), s8[2097152]{0:T(1024)(128)(4,1)S(1)}, s32[]{:S(2)}) async-start(s8[6291456]{0:T(1024)(128)(4,1)} %bitcast.37), calls=%async_computation.8 | async-start | bytes 4194304
  270.1 8.0 %copy-start.1 = (f32[2,256,256]{2,1,0:T(8,128)S(1)}, f32[2,256,256]{2,1,0:T(8,128)}, u32[]{:S(2)}) copy-start(f32[2,256,256]{2,1,0:T(8,128)} %fusion) | copy-start | bytes 1572868
  270.1 8.5 %slice-start.1 = ((s8[6291456]{0:T(1024)(128)(4,1)}), s8[4194304]{0:T(1024)(128)(4,1)S(1)}, s32[]{:S(2)}) async-start(s8[6291456]{0:T(1024)(128)(4,1)} %bitcast.37), calls=%async_computation.9 | async-start | bytes 8388608
  278.6 17.8 %copy-start.2 = (f32[2]{0:T(128)S(1)}, f32[2]{0:T(128)}, u32[]{:S(2)}) copy-start(f32[2]{0:T(128)} %param.9) | copy-start | bytes 28
  329.3 73.7 %all-to-all-start.2 = ((bf16[4,384,1536]{2,1,0:T(8,128)(2,1)}), bf16[4,384,1536]{2,1,0:T(8,128)(2,1)}, u32[]{:S(2)}, u32[]{:S(2)}) async-start(bf16[4,384,1536]{2,1,0:T(8,128)(2,1)} %bitcast.41), calls=%async_computation.3 | async-start | bytes 9437184 | tf_op jit(solution)/shard_map/all_to_all | solution.py:41
Sparse Core Ops, SparseCore 0:
  10.8 84.6 all-gather.3
  99.7 56.0 all-gather.7
  157.6 55.5 all-gather.5
  305.0 61.6 reduce-scatter.1
